TPU v7x, 1024 devices: a whole 4x4x32 slice. The times are simulated.
1024 devices in a mesh: section: 16 (over x, y), seq: 64 (over z, core).
Axes of the slice: x: 4, y: 4, z: 32, core: 2. Of those that a mesh axis runs over, the one named last changes fastest.
Arguments:
- grad_out: bfloat16 [16, 4096, 8192], P('section', 'seq'), may hold values from -6 to 6
- step_sizes: float32 [16, 128, 8192], P('section', None, 'seq'), may hold values from 0.01 to 0.1
- decay_rate: float32 [16, 128], P('section', 'seq'), may hold values from 0.001 to 1
- skip_gain: float32 [16, 128], P('section', 'seq'), may hold values from 0.5 to 1.5
- state_in: bfloat16 [16, 8, 8192, 128], P('section', None, 'seq'), may hold values from -6 to 6
- state_out: bfloat16 [16, 8, 8192, 128], P('section', None, 'seq'), may hold values from -0.5 to 0.5
- segment_ids: int32 [16, 8192], P('section'), may hold values from 0 to 15, never falling along the last dimension, each value on 1 to 4096 neighbouring positions
Outputs:
- incoming: bfloat16 [16, 4096, 8192], P('section', 'seq')
All inputs are finite; a program needn't handle non-finite values.
Results may differ from a plain program's by a relative error of at most 0.007.
Values may be sent and summed in bfloat16 or wider, within the bound.
No kernel may reach another device: no remote copies, remote signals or barrier semaphores. Data moves between devices by JAX's collectives and lax.ppermute only.
A program may use at most 32 MiB of HBM per device.

v0:
```python
import functools

import jax
import jax.numpy as jnp
from jax import lax
from jax.experimental import pallas as pl
from jax.experimental.pallas import tpu as pltpu
from jax.sharding import PartitionSpec as P


SPAN = 256
HALF = 128
STATE = 128
SPANS = 32
GROUPS = 8
LEVELS = 4
DOCS = 16
STEP_ROWS = 16
SLAB = 2 * HALF + STEP_ROWS
UNROLL = 4
BASE = (0, 2, 13, 21, 22, 20, 12, 1)
COUNT = (3, 3, 2, 3, 3, 3, 2, 3)
FIRST = (0, 12, 20)
F32 = jnp.float32
BF16 = jnp.bfloat16


def core_kernel(seq, place, small_ref, grad_ref, *refs):
    parts, (out_ref, slabs, dt_ref, grow_ref, shrink_ref, carry_ref, keep_ref, fac_ref, end_ref, local_ref, right_ref, sems) = (
        refs[:6],
        refs[6:],
    )
    seq = lax.axis_index("seq") if seq is None else seq
    group, level, core = seq // 8, (seq // 2) % 4, seq % 2
    copies = []
    for number, part in enumerate(parts):
        copies.append(
            pltpu.make_async_copy(
                part,
                slabs.at[number // 3, pl.ds(FIRST[number % 3], part.shape[0])],
                sems.at[number],
            )
        )
    for copy in copies:
        copy.start()

    seg = small_ref[:SPANS, :].astype(jnp.int32)
    last = jnp.broadcast_to(seg[:, SPAN - 1 : SPAN], seg.shape)
    before = jnp.concatenate([last[:1], last[:-1]], axis=0)
    end = jnp.zeros_like(seg)
    for doc in range(DOCS):
        end = jnp.where(seg == doc, jnp.sum((seg <= doc).astype(jnp.int32)), end)
    own = lax.broadcasted_iota(jnp.int32, seg.shape, 0) * SPAN
    end_ref[...] = end - own
    kept = (seg == before).astype(F32)
    at_end = (seg == last).astype(F32)
    joined = (last == before).astype(F32)

    for copy in copies:
        copy.wait()

    def where_is(span):
        step = (span // LEVELS - group) & (GROUPS - 1)
        return place[step] + ((span % LEVELS) ^ level) * place[GROUPS + step]

    first_head = 4 * level + 2 * core
    row = lax.broadcasted_iota(jnp.int32, (STEP_ROWS, HALF), 0)

    for span in range(SPANS):
        at_slab = where_is(span)
        for half in range(2):
            tile = slabs[half ^ core, at_slab, 2 * HALF :, :].astype(F32)
            for head in range(2):
                picked = jnp.sum(
                    jnp.where(row == first_head + head, tile, 0.0), axis=0, keepdims=True
                )
                at = head * SPANS + span
                dt_ref[at : at + 1, half * HALF : (half + 1) * HALF] = picked
    ahead = (
        lax.broadcasted_iota(jnp.int32, (SPAN, SPAN), 0)
        <= lax.broadcasted_iota(jnp.int32, (SPAN, SPAN), 1)
    ).astype(F32).astype(BF16)
    dt = dt_ref[...]
    summed = jnp.dot(dt.astype(BF16), ahead, preferred_element_type=F32)
    for head in range(2):
        rows = slice(head * SPANS, (head + 1) * SPANS)
        within = -small_ref[SPANS + head : SPANS + head + 1, :] * summed[rows]
        total = jnp.broadcast_to(within[:, SPAN - 1 : SPAN], within.shape)
        grow = jnp.exp(within)
        grow_ref[rows, :] = grow
        keep_ref[rows, :] = kept
        shrink_ref[rows, :] = dt[rows] * jnp.exp(-within)
        carry_ref[rows, :] = dt[rows] * at_end * jnp.exp(total - within)
        fac_ref[rows, :] = (joined * jnp.exp(total))[:, :STATE]

    def both(ref, span, lanes):
        return jnp.concatenate(
            [
                jnp.broadcast_to(ref[pl.ds(head * SPANS + span, 1), :], (32, lanes))
                for head in range(2)
            ],
            axis=0,
        )

    def grown(span):
        grad = grad_ref[:, pl.ds(pl.multiple_of(span * SPAN, SPAN), SPAN)].astype(F32)
        return grad, (grad * both(grow_ref, span, SPAN))

    def rows_of(span, first):
        at_slab = where_is(span)
        return jnp.concatenate(
            [slabs[half ^ core, at_slab, first : first + HALF, :] for half in range(2)],
            axis=0,
        )

    def local_of(span, _):
        _, scaled = grown(span)
        masked = (scaled * both(keep_ref, span, SPAN)).astype(BF16)
        local_ref[span] = jnp.dot(masked, rows_of(span, HALF), preferred_element_type=F32)
        return 0

    lax.fori_loop(0, SPANS, local_of, 0, unroll=UNROLL)

    def recur(number, state):
        span = SPANS - 1 - number
        high = state.astype(BF16)
        right_ref[span, 0:64, :] = high
        right_ref[span, 64:128, :] = (state - high.astype(F32)).astype(BF16)
        return local_ref[span] + both(fac_ref, span, STATE) * state

    lax.fori_loop(0, SPANS, recur, jnp.zeros((64, STATE), F32), unroll=UNROLL)
    behind = (
        lax.broadcasted_iota(jnp.int32, (HALF, HALF), 0)
        >= lax.broadcasted_iota(jnp.int32, (HALF, HALF), 1)
    )
    token = lax.broadcasted_iota(jnp.int32, (HALF, HALF), 0)
    gains = jnp.concatenate(
        [
            jnp.broadcast_to(small_ref[SPANS + 2 + head : SPANS + 3 + head, :], (32, SPAN))
            for head in range(2)
        ],
        axis=0,
    )
    nt = (((1,), (1,)), ((), ()))

    def span_of(span, _):
        writes = rows_of(span, 0)
        reads = rows_of(span, HALF)
        grad, scaled = grown(span)
        scaled = scaled.astype(BF16)
        left = jnp.concatenate([reads, right_ref[span]], axis=0)
        product = lax.dot_general(left, writes, nt, preferred_element_type=F32)
        carried = product[SPAN : SPAN + 64] + product[SPAN + 64 :]
        end = end_ref[pl.ds(span, 1), :]
        first_end, second_end = end[:, :HALF], end[:, HALF:]
        s00 = jnp.where(behind & (token < first_end), product[:HALF, :HALF], 0.0).astype(BF16)
        s10 = jnp.where(token + HALF < first_end, product[HALF:SPAN, :HALF], 0.0).astype(BF16)
        s11 = jnp.where(
            behind & (token + HALF < second_end), product[HALF:SPAN, HALF:], 0.0
        ).astype(BF16)
        zero = jnp.zeros((HALF, HALF), BF16)
        scores = jnp.concatenate(
            [jnp.concatenate([s00, zero], axis=1), jnp.concatenate([s10, s11], axis=1)], axis=0
        )
        inner = jnp.dot(scaled, scores, preferred_element_type=F32)
        out = (
            both(shrink_ref, span, SPAN) * inner
            + both(carry_ref, span, SPAN) * carried
            + gains * grad
        )
        out_ref[:, pl.ds(pl.multiple_of(span * SPAN, SPAN), SPAN)] = out.astype(BF16)
        return 0

    lax.fori_loop(0, SPANS, span_of, 0, unroll=UNROLL)


def core_call(small, grad, parts, seq=None, interpret=False):
    smem = pl.BlockSpec(memory_space=pltpu.SMEM)
    vmem = pl.BlockSpec(memory_space=pltpu.VMEM)
    return pl.pallas_call(
        functools.partial(core_kernel, seq),
        out_shape=jax.ShapeDtypeStruct(grad.shape, BF16),
        in_specs=[smem, vmem, vmem] + [pl.BlockSpec(memory_space=pl.ANY)] * 6,
        out_specs=vmem,
        scratch_shapes=[
            pltpu.VMEM((2, SPANS, SLAB, STATE), BF16),
            pltpu.VMEM((2 * SPANS, SPAN), F32),
            pltpu.VMEM((2 * SPANS, SPAN), F32),
            pltpu.VMEM((2 * SPANS, SPAN), F32),
            pltpu.VMEM((2 * SPANS, SPAN), F32),
            pltpu.VMEM((2 * SPANS, SPAN), F32),
            pltpu.VMEM((2 * SPANS, STATE), F32),
            pltpu.VMEM((SPANS, SPAN), jnp.int32),
            pltpu.VMEM((SPANS, 64, STATE), F32),
            pltpu.VMEM((SPANS, 128, STATE), BF16),
            pltpu.SemaphoreType.DMA((6,)),
        ],
        compiler_params=pltpu.CompilerParams(vmem_limit_bytes=24 * 1024 * 1024),
        interpret=interpret,
        name="span_grads",
    )(jnp.array(BASE + COUNT, jnp.int32), small, grad, *parts)


def shift_pairs(of):
    pairs = []
    for section in range(16):
        for group in range(GROUPS):
            for level in range(LEVELS):
                for core in range(2):
                    target = of(section, group, level, core)
                    if target is not None and target[0] >= 0:
                        there = target[1] % GROUPS * 8 + target[2] * 2 + target[3]
                        pairs.append((section * 64 + group * 8 + level * 2 + core, target[0] * 64 + there))
    return pairs


def moved(value, of):
    return lax.ppermute(value, ("section", "seq"), shift_pairs(of))


def to_group(value, distance):
    return moved(value, lambda s, g, k, c: (s - 1, g + distance, k, c))


def onward(value, distance):
    return moved(value, lambda s, g, k, c: (s, g + distance, k, c))


def levels(value, steps):
    return moved(value, lambda s, g, k, c: (s, g, steps[k], c) if k in steps else None)


def group_gather(chunk, outer):
    middle, ends = {1: 2, 2: 1}, {1: 0, 2: 3}
    near = levels(chunk, {0: 1, 1: 0, 2: 3, 3: 2})
    across = levels(chunk, middle)
    far = levels(near, middle)
    end_near = levels(across, ends)
    end_far = levels(far, ends)
    chunk, near, across, far, end_near, end_far = lax.optimization_barrier(
        (chunk, near, across, far, end_near, end_far)
    )
    every = jnp.concatenate(
        [chunk, near, jnp.where(outer, end_near, far), jnp.where(outer, end_far, across)], axis=0
    )
    other = moved(every, lambda s, g, k, c: (s, g, k, c ^ 1))
    return every.reshape(-1, SLAB, STATE), other.reshape(-1, SLAB, STATE)


def local(grad_out, step_sizes, decay_rate, skip_gain, state_in, state_out, segment_ids):
    seq = lax.axis_index("seq")
    group, level = seq // 8, seq // 2 % 4
    steps = step_sizes[0].astype(BF16).reshape(GROUPS, STEP_ROWS, HALF)
    slab = jnp.concatenate([state_in[0], state_out[0], steps], axis=1)

    def slab_for(distance):
        return lax.dynamic_index_in_dim(slab, (group + distance) % GROUPS, 0, False)

    far = slab_for(4)
    right_1 = to_group(jnp.concatenate([slab_for(1), slab_for(3)]), 1)
    left_1 = to_group(jnp.concatenate([slab_for(7), slab_for(5)]), -1)
    right_2 = to_group(jnp.concatenate([slab_for(2), far[:HALF]]), 2)
    left_2 = to_group(jnp.concatenate([slab_for(6), far[HALF:]]), -2)
    own = to_group(slab_for(0), 0)
    grad = to_group(grad_out[0], 0)
    small = jnp.concatenate(
        [
            segment_ids[0].reshape(SPANS, SPAN).astype(F32),
            jnp.broadcast_to(jnp.concatenate([decay_rate[0], skip_gain[0]])[:, None], (4, SPAN)),
            jnp.zeros((4, SPAN), F32),
        ],
        axis=0,
    )
    small = to_group(small, 0)
    first_in = jnp.concatenate([own, right_1[:SLAB], left_1[:SLAB]])
    right_in = jnp.concatenate([right_1[SLAB:], right_2[SLAB:]])
    left_in = jnp.concatenate([left_1[SLAB:], left_2[SLAB:]])
    second_in = jnp.concatenate([right_2[:SLAB], left_2[:SLAB]])
    right_3 = onward(right_in, 2)
    left_3 = onward(left_in, -2)
    third_in = jnp.concatenate([right_3[:SLAB], left_3[:SLAB], right_3[SLAB:], left_3[SLAB:]])
    outer = (level == 0) | (level == 3)
    first, first_other = group_gather(first_in, outer)
    second, second_other = group_gather(second_in, outer)
    third, third_other = group_gather(third_in, outer)
    out = core_call(
        small, grad, (first, second, third, first_other, second_other, third_other)
    )
    return out[None]


def solution(mesh):
    placed = (
        P("section", "seq", None),
        P("section", None, "seq"),
        P("section", "seq"),
        P("section", "seq"),
        P("section", None, "seq", None),
        P("section", None, "seq", None),
        P("section", None),
    )
    return jax.shard_map(
        local, mesh=mesh, in_specs=placed, out_specs=P("section", "seq", None), check_vma=False
    )
```

profile of v0, /device:TPU:14, one launch (start us, length us, event | category | flops | bytes accessed | tf_op | source)
XLA Modules:
  0.0 166.4 jit_solution(11886144715860012465)
XLA Ops:
  0.8 1.1 pad_maximum_fusion.2
  2.0 2.4 %collective-permute-start.2 = (bf16[272,128]{1,0:T(8,128)(2,1)S(1)}, bf16[272,128]{1,0:T(8,128)(2,1)S(1)}, u32[]{:S(2)}, u32[]{:S(2)}) collective-permute-start(bf16[272,128]{1,0:T(8,128)(2,1)S(1)} %get-tuple-element.47), channel_id=1, source_target_pairs={{64,0},{65,1},{66,2},{67,3},{68,4},{69,5},{70,6},{71,7},{72,8},{73... | collective-permute-start | bytes 208904 | tf_op jit(solution)/shard_map/ppermute | solution.py:218
  4.4 18.4 %collective-permute-start.10 = (bf16[400,128]{1,0:T(8,128)(2,1)S(1)}, bf16[400,128]{1,0:T(8,128)(2,1)S(1)}, u32[]{:S(2)}, u32[]{:S(2)}) collective-permute-start(bf16[400,128]{1,0:T(8,128)(2,1)S(1)} %pad_maximum_fusion.11), channel_id=1, source_target_pairs={{64,16},{65,17},{66,18},{67,19},{68,20},{69,21},{70,22},{71,23},{7... | collective-permute-start | bytes 307208 | tf_op jit(solution)/shard_map/ppermute | solution.py:218
  22.9 9.2 %collective-permute-start.11 = (bf16[416,128]{1,0:T(8,128)(2,1)S(1)}, bf16[416,128]{1,0:T(8,128)(2,1)S(1)}, u32[]{:S(2)}, u32[]{:S(2)}) collective-permute-start(bf16[416,128]{1,0:T(8,128)(2,1)S(1)} %pad_maximum_fusion.9), channel_id=1, source_target_pairs={{64,48},{65,49},{66,50},{67,51},{68,52},{69,53},{70,54},{71,55},{7... | collective-permute-start | bytes 319496 | tf_op jit(solution)/shard_map/ppermute | solution.py:218
  32.1 4.5 %collective-permute-start.3 = (bf16[544,128]{1,0:T(8,128)(2,1)S(1)}, bf16[544,128]{1,0:T(8,128)(2,1)S(1)}, u32[]{:S(2)}, u32[]{:S(2)}) collective-permute-start(bf16[544,128]{1,0:T(8,128)(2,1)S(1)} %pad_maximum_fusion.6), channel_id=1, source_target_pairs={{64,8},{65,9},{66,10},{67,11},{68,12},{69,13},{70,14},{71,15},{72,... | collective-permute-start | bytes 417800 | tf_op jit(solution)/shard_map/ppermute | solution.py:218
  36.6 7.2 %collective-permute-start.4 = (bf16[544,128]{1,0:T(8,128)(2,1)S(1)}, bf16[544,128]{1,0:T(8,128)(2,1)S(1)}, u32[]{:S(2)}, u32[]{:S(2)}) collective-permute-start(bf16[544,128]{1,0:T(8,128)(2,1)S(1)} %pad_maximum_fusion.7), channel_id=1, source_target_pairs={{64,56},{65,57},{66,58},{67,59},{68,60},{69,61},{70,62},{71,63},{7... | collective-permute-start | bytes 417800 | tf_op jit(solution)/shard_map/ppermute | solution.py:218
  43.8 20.0 %collective-permute-done.11 = bf16[416,128]{1,0:T(8,128)(2,1)S(1)} collective-permute-done((bf16[416,128]{1,0:T(8,128)(2,1)S(1)}, bf16[416,128]{1,0:T(8,128)(2,1)S(1)}, u32[]{:S(2)}, u32[]{:S(2)}) %collective-permute-start.11) | collective-permute-done | bytes 106528 | tf_op jit(solution)/shard_map/ppermute | solution.py:218
  63.8 1.9 %collective-permute-start.12 = (bf16[544,128]{1,0:T(8,128)(2,1)S(1)}, bf16[544,128]{1,0:T(8,128)(2,1)S(1)}, u32[]{:S(2)}, u32[]{:S(2)}) collective-permute-start(bf16[544,128]{1,0:T(8,128)(2,1)S(1)} %pad_maximum_fusion.8), channel_id=1, source_target_pairs={{0,2},{1,3},{2,0},{3,1},{4,6},{5,7},{6,4},{7,5},{8,10},{9,11},{10,... | collective-permute-start | bytes 417800 | tf_op jit(solution)/shard_map/ppermute | solution.py:218
  65.8 10.9 %collective-permute-start.17 = (bf16[400,128]{1,0:T(8,128)(2,1)S(1)}, bf16[400,128]{1,0:T(8,128)(2,1)S(1)}, u32[]{:S(2)}, u32[]{:S(2)}) collective-permute-start(bf16[400,128]{1,0:T(8,128)(2,1)S(1)} %pad_maximum_fusion.12), channel_id=1, source_target_pairs={{0,16},{1,17},{2,18},{3,19},{4,20},{5,21},{6,22},{7,23},{8,24},{9,... | collective-permute-start | bytes 307208 | tf_op jit(solution)/shard_map/ppermute | solution.py:218
  76.8 3.7 %collective-permute-start.18 = (bf16[416,128]{1,0:T(8,128)(2,1)S(1)}, bf16[416,128]{1,0:T(8,128)(2,1)S(1)}, u32[]{:S(2)}, u32[]{:S(2)}) collective-permute-start(bf16[416,128]{1,0:T(8,128)(2,1)S(1)} %pad_maximum_fusion.10), channel_id=1, source_target_pairs={{0,48},{1,49},{2,50},{3,51},{4,52},{5,53},{6,54},{7,55},{8,56},{9,... | collective-permute-start | bytes 319496 | tf_op jit(solution)/shard_map/ppermute | solution.py:218
  80.5 3.9 %collective-permute-start.5 = (bf16[816,128]{1,0:T(8,128)(2,1)S(1)}, bf16[816,128]{1,0:T(8,128)(2,1)S(1)}, u32[]{:S(2)}, u32[]{:S(2)}) collective-permute-start(bf16[816,128]{1,0:T(8,128)(2,1)S(1)} %pad_maximum_fusion.4), channel_id=1, source_target_pairs={{0,2},{1,3},{2,0},{3,1},{4,6},{5,7},{6,4},{7,5},{8,10},{9,11},{10,... | collective-permute-start | bytes 626696 | tf_op jit(solution)/shard_map/ppermute | solution.py:218
  85.1 1.0 collective-permute-done.17
  86.8 6.2 %collective-permute-done.18 = bf16[416,128]{1,0:T(8,128)(2,1)S(1)} collective-permute-done((bf16[416,128]{1,0:T(8,128)(2,1)S(1)}, bf16[416,128]{1,0:T(8,128)(2,1)S(1)}, u32[]{:S(2)}, u32[]{:S(2)}) %collective-permute-start.18) | collective-permute-done | bytes 106528 | tf_op jit(solution)/shard_map/ppermute | solution.py:218
  93.8 1.3 collective-permute-start.20
  95.1 14.4 %collective-permute-start.19 = (bf16[816,128]{1,0:T(8,128)(2,1)S(1)}, bf16[816,128]{1,0:T(8,128)(2,1)S(1)}, u32[]{:S(2)}, u32[]{:S(2)}) collective-permute-start(bf16[816,128]{1,0:T(8,128)(2,1)S(1)} %pad_maximum_fusion.5), channel_id=1, source_target_pairs={{0,2},{1,3},{2,0},{3,1},{4,6},{5,7},{6,4},{7,5},{8,10},{9,11},{10,... | collective-permute-start | bytes 626696 | tf_op jit(solution)/shard_map/ppermute | solution.py:218
  110.2 1.3 collective-permute-start.15
  111.5 1.3 collective-permute-start.16
  112.9 5.7 %collective-permute-done.15 = bf16[544,128]{1,0:T(8,128)(2,1)S(1)} collective-permute-done((bf16[544,128]{1,0:T(8,128)(2,1)S(1)}, bf16[544,128]{1,0:T(8,128)(2,1)S(1)}, u32[]{:S(2)}, u32[]{:S(2)}) %collective-permute-start.15) | collective-permute-done | bytes 139296 | tf_op jit(solution)/shard_map/ppermute | solution.py:218
  118.5 4.8 %collective-permute-start.1 = (bf16[64,8192]{1,0:T(8,128)(2,1)}, bf16[64,8192]{1,0:T(8,128)(2,1)S(1)}, u32[]{:S(2)}, u32[]{:S(2)}) collective-permute-start(bf16[64,8192]{1,0:T(8,128)(2,1)} %bitcast.37), channel_id=1, source_target_pairs={{64,0},{65,1},{66,2},{67,3},{68,4},{69,5},{70,6},{71,7},{72,8},{73... | collective-permute-start | bytes 3145736 | tf_op jit(solution)/shard_map/ppermute | solution.py:218
  123.3 1.3 collective-permute-start.8
  124.7 1.3 collective-permute-start.22
  126.7 1.3 collective-permute-start.9
  128.0 1.3 collective-permute-start.23
  129.3 1.7 %collective-permute-done.8 = bf16[816,128]{1,0:T(8,128)(2,1)S(1)} collective-permute-done((bf16[816,128]{1,0:T(8,128)(2,1)S(1)}, bf16[816,128]{1,0:T(8,128)(2,1)S(1)}, u32[]{:S(2)}, u32[]{:S(2)}) %collective-permute-start.8) | collective-permute-done | bytes 208928 | tf_op jit(solution)/shard_map/ppermute | solution.py:218
  131.0 4.6 %collective-permute-done.9 = bf16[816,128]{1,0:T(8,128)(2,1)S(1)} collective-permute-done((bf16[816,128]{1,0:T(8,128)(2,1)S(1)}, bf16[816,128]{1,0:T(8,128)(2,1)S(1)}, u32[]{:S(2)}, u32[]{:S(2)}) %collective-permute-start.9) | collective-permute-done | bytes 208928 | tf_op jit(solution)/shard_map/ppermute | solution.py:218
  135.8 1.9 %collective-permute-start.24 = (bf16[3264,128]{1,0:T(8,128)(2,1)S(1)}, bf16[3264,128]{1,0:T(8,128)(2,1)}, u32[]{:S(2)}, u32[]{:S(2)}) collective-permute-start(bf16[3264,128]{1,0:T(8,128)(2,1)S(1)} %pad_maximum_fusion), channel_id=1, source_target_pairs={{0,1},{1,0},{2,3},{3,2},{4,5},{5,4},{6,7},{7,6},{8,9},{9,8},{10,11... | collective-permute-start | bytes 2506760 | tf_op jit(solution)/shard_map/ppermute | solution.py:218
  137.7 3.6 %collective-permute-done.23 = bf16[816,128]{1,0:T(8,128)(2,1)S(1)} collective-permute-done((bf16[816,128]{1,0:T(8,128)(2,1)S(1)}, bf16[816,128]{1,0:T(8,128)(2,1)S(1)}, u32[]{:S(2)}, u32[]{:S(2)}) %collective-permute-start.23) | collective-permute-done | bytes 208928 | tf_op jit(solution)/shard_map/ppermute | solution.py:218
  141.6 2.1 %collective-permute-start.26 = (bf16[3264,128]{1,0:T(8,128)(2,1)S(1)}, bf16[3264,128]{1,0:T(8,128)(2,1)}, u32[]{:S(2)}, u32[]{:S(2)}) collective-permute-start(bf16[3264,128]{1,0:T(8,128)(2,1)S(1)} %pad_maximum_fusion.1), channel_id=1, source_target_pairs={{0,1},{1,0},{2,3},{3,2},{4,5},{5,4},{6,7},{7,6},{8,9},{9,8},{10,11... | collective-permute-start | bytes 2506760 | tf_op jit(solution)/shard_map/ppermute | solution.py:218
  143.7 2.4 %collective-permute-start.25 = (bf16[2176,128]{1,0:T(8,128)(2,1)S(1)}, bf16[2176,128]{1,0:T(8,128)(2,1)}, u32[]{:S(2)}, u32[]{:S(2)}) collective-permute-start(bf16[2176,128]{1,0:T(8,128)(2,1)S(1)} %pad_maximum_fusion.3), channel_id=1, source_target_pairs={{0,1},{1,0},{2,3},{3,2},{4,5},{5,4},{6,7},{7,6},{8,9},{9,8},{10,11... | collective-permute-start | bytes 1671176 | tf_op jit(solution)/shard_map/ppermute | solution.py:218
  146.5 1.9 %collective-permute-start = (f32[40,256]{1,0:T(8,128)S(1)}, f32[40,256]{1,0:T(8,128)S(1)}, u32[]{:S(2)}, u32[]{:S(2)}) collective-permute-start(f32[40,256]{1,0:T(8,128)S(1)} %maximum_maximum_fusion), channel_id=1, source_target_pairs={{64,0},{65,1},{66,2},{67,3},{68,4},{69,5},{70,6},{71,7},{72,8},{73... | collective-permute-start | bytes 122888 | tf_op jit(solution)/shard_map/ppermute | solution.py:218
  148.4 4.0 %collective-permute-done.small_ref = f32[40,256]{1,0:T(8,128)S(1)} collective-permute-done((f32[40,256]{1,0:T(8,128)S(1)}, f32[40,256]{1,0:T(8,128)S(1)}, u32[]{:S(2)}, u32[]{:S(2)}) %collective-permute-start) | collective-permute-done | bytes 40992 | tf_op jit(solution)/shard_map/ppermute | solution.py:218
  152.4 14.0 %span_grads.1 = bf16[64,8192]{1,0:T(8,128)(2,1)} custom-call(s32[16]{0:T(128)S(1)} %copy-done, f32[40,256]{1,0:T(8,128)S(1)} %collective-permute-done.small_ref, bf16[64,8192]{1,0:T(8,128)(2,1)S(1)} %collective-permute-done.1.grad_ref, bf16[12,272,128]{2,1,0:T(8,128)(2,1)S(1)} %bitcast.31, bf16[8,272,128]{2,1,0:T(8,128)(2,1)S(1)} %bitcast.33, ...), custom_call_target="tpu_custom_call" | custom-call | tf_op jit(solution)/shard_map/span_grads/pallas_call | solution.py:180
  (79 shorter events, 5.2 us)
Async XLA Ops:
  2.0 78.5 %collective-permute-start.2 = (bf16[272,128]{1,0:T(8,128)(2,1)S(1)}, bf16[272,128]{1,0:T(8,128)(2,1)S(1)}, u32[]{:S(2)}, u32[]{:S(2)}) collective-permute-start(bf16[272,128]{1,0:T(8,128)(2,1)S(1)} %get-tuple-element.47), channel_id=1, source_target_pairs={{64,0},{65,1},{66,2},{67,3},{68,4},{69,5},{70,6},{71,7},{72,8},{73... | collective-permute-start | bytes 208904 | tf_op jit(solution)/shard_map/ppermute | solution.py:218
  4.4 39.4 %collective-permute-start.10 = (bf16[400,128]{1,0:T(8,128)(2,1)S(1)}, bf16[400,128]{1,0:T(8,128)(2,1)S(1)}, u32[]{:S(2)}, u32[]{:S(2)}) collective-permute-start(bf16[400,128]{1,0:T(8,128)(2,1)S(1)} %pad_maximum_fusion.11), channel_id=1, source_target_pairs={{64,16},{65,17},{66,18},{67,19},{68,20},{69,21},{70,22},{71,23},{7... | collective-permute-start | bytes 307208 | tf_op jit(solution)/shard_map/ppermute | solution.py:218
  22.9 40.9 %collective-permute-start.11 = (bf16[416,128]{1,0:T(8,128)(2,1)S(1)}, bf16[416,128]{1,0:T(8,128)(2,1)S(1)}, u32[]{:S(2)}, u32[]{:S(2)}) collective-permute-start(bf16[416,128]{1,0:T(8,128)(2,1)S(1)} %pad_maximum_fusion.9), channel_id=1, source_target_pairs={{64,48},{65,49},{66,50},{67,51},{68,52},{69,53},{70,54},{71,55},{7... | collective-permute-start | bytes 319496 | tf_op jit(solution)/shard_map/ppermute | solution.py:218
  32.1 33.7 %collective-permute-start.3 = (bf16[544,128]{1,0:T(8,128)(2,1)S(1)}, bf16[544,128]{1,0:T(8,128)(2,1)S(1)}, u32[]{:S(2)}, u32[]{:S(2)}) collective-permute-start(bf16[544,128]{1,0:T(8,128)(2,1)S(1)} %pad_maximum_fusion.6), channel_id=1, source_target_pairs={{64,8},{65,9},{66,10},{67,11},{68,12},{69,13},{70,14},{71,15},{72,... | collective-permute-start | bytes 417800 | tf_op jit(solution)/shard_map/ppermute | solution.py:218
  36.6 40.1 %collective-permute-start.4 = (bf16[544,128]{1,0:T(8,128)(2,1)S(1)}, bf16[544,128]{1,0:T(8,128)(2,1)S(1)}, u32[]{:S(2)}, u32[]{:S(2)}) collective-permute-start(bf16[544,128]{1,0:T(8,128)(2,1)S(1)} %pad_maximum_fusion.7), channel_id=1, source_target_pairs={{64,56},{65,57},{66,58},{67,59},{68,60},{69,61},{70,62},{71,63},{7... | collective-permute-start | bytes 417800 | tf_op jit(solution)/shard_map/ppermute | solution.py:218
  63.8 29.9 %copy-start.1 = (bf16[544,128]{1,0:T(8,128)(2,1)}, bf16[544,128]{1,0:T(8,128)(2,1)S(1)}, u32[]{:S(2)}) copy-start(bf16[544,128]{1,0:T(8,128)(2,1)S(1)} %pad_maximum_fusion.8) | copy-start | bytes 417796
  63.8 29.2 %collective-permute-start.12 = (bf16[544,128]{1,0:T(8,128)(2,1)S(1)}, bf16[544,128]{1,0:T(8,128)(2,1)S(1)}, u32[]{:S(2)}, u32[]{:S(2)}) collective-permute-start(bf16[544,128]{1,0:T(8,128)(2,1)S(1)} %pad_maximum_fusion.8), channel_id=1, source_target_pairs={{0,2},{1,3},{2,0},{3,1},{4,6},{5,7},{6,4},{7,5},{8,10},{9,11},{10,... | collective-permute-start | bytes 417800 | tf_op jit(solution)/shard_map/ppermute | solution.py:218
  65.8 20.3 %collective-permute-start.17 = (bf16[400,128]{1,0:T(8,128)(2,1)S(1)}, bf16[400,128]{1,0:T(8,128)(2,1)S(1)}, u32[]{:S(2)}, u32[]{:S(2)}) collective-permute-start(bf16[400,128]{1,0:T(8,128)(2,1)S(1)} %pad_maximum_fusion.12), channel_id=1, source_target_pairs={{0,16},{1,17},{2,18},{3,19},{4,20},{5,21},{6,22},{7,23},{8,24},{9,... | collective-permute-start | bytes 307208 | tf_op jit(solution)/shard_map/ppermute | solution.py:218
  76.8 16.3 %collective-permute-start.18 = (bf16[416,128]{1,0:T(8,128)(2,1)S(1)}, bf16[416,128]{1,0:T(8,128)(2,1)S(1)}, u32[]{:S(2)}, u32[]{:S(2)}) collective-permute-start(bf16[416,128]{1,0:T(8,128)(2,1)S(1)} %pad_maximum_fusion.10), channel_id=1, source_target_pairs={{0,48},{1,49},{2,50},{3,51},{4,52},{5,53},{6,54},{7,55},{8,56},{9,... | collective-permute-start | bytes 319496 | tf_op jit(solution)/shard_map/ppermute | solution.py:218
  80.5 29.0 %collective-permute-start.5 = (bf16[816,128]{1,0:T(8,128)(2,1)S(1)}, bf16[816,128]{1,0:T(8,128)(2,1)S(1)}, u32[]{:S(2)}, u32[]{:S(2)}) collective-permute-start(bf16[816,128]{1,0:T(8,128)(2,1)S(1)} %pad_maximum_fusion.4), channel_id=1, source_target_pairs={{0,2},{1,3},{2,0},{3,1},{4,6},{5,7},{6,4},{7,5},{8,10},{9,11},{10,... | collective-permute-start | bytes 626696 | tf_op jit(solution)/shard_map/ppermute | solution.py:218
  84.4 25.8 %collective-permute-start.6 = (bf16[816,128]{1,0:T(8,128)(2,1)S(1)}, bf16[816,128]{1,0:T(8,128)(2,1)S(1)}, u32[]{:S(2)}, u32[]{:S(2)}) collective-permute-start(bf16[816,128]{1,0:T(8,128)(2,1)S(1)} %pad_maximum_fusion.4), channel_id=1, source_target_pairs={{2,4},{3,5},{4,2},{5,3},{10,12},{11,13},{12,10},{13,11},{18,20},{1... | collective-permute-start | bytes 626696 | tf_op jit(solution)/shard_map/ppermute | solution.py:218
  86.1 9.0 %collective-permute-start.13 = (bf16[544,128]{1,0:T(8,128)(2,1)S(1)}, bf16[544,128]{1,0:T(8,128)(2,1)S(1)}, u32[]{:S(2)}, u32[]{:S(2)}) collective-permute-start(bf16[544,128]{1,0:T(8,128)(2,1)S(1)} %pad_maximum_fusion.8), channel_id=1, source_target_pairs={{2,4},{3,5},{4,2},{5,3},{10,12},{11,13},{12,10},{13,11},{18,20},{1... | collective-permute-start | bytes 417800 | tf_op jit(solution)/shard_map/ppermute | solution.py:218
  93.1 33.6 %copy-start.5 = (bf16[544,128]{1,0:T(8,128)(2,1)}, bf16[544,128]{1,0:T(8,128)(2,1)S(1)}, u32[]{:S(2)}) copy-start(bf16[544,128]{1,0:T(8,128)(2,1)S(1)} %collective-permute-done.12) | copy-start | bytes 417796
  93.1 18.5 %collective-permute-start.14 = (bf16[544,128]{1,0:T(8,128)(2,1)S(1)}, bf16[544,128]{1,0:T(8,128)(2,1)S(1)}, u32[]{:S(2)}, u32[]{:S(2)}) collective-permute-start(bf16[544,128]{1,0:T(8,128)(2,1)S(1)} %collective-permute-done.12), channel_id=1, source_target_pairs={{2,4},{3,5},{4,2},{5,3},{10,12},{11,13},{12,10},{13,11},{18,20},{1... | collective-permute-start | bytes 417800 | tf_op jit(solution)/shard_map/ppermute | solution.py:218
  93.8 29.6 %collective-permute-start.20 = (bf16[816,128]{1,0:T(8,128)(2,1)S(1)}, bf16[816,128]{1,0:T(8,128)(2,1)}, u32[]{:S(2)}, u32[]{:S(2)}) collective-permute-start(bf16[816,128]{1,0:T(8,128)(2,1)S(1)} %pad_maximum_fusion.5), channel_id=1, source_target_pairs={{2,4},{3,5},{4,2},{5,3},{10,12},{11,13},{12,10},{13,11},{18,20},{1... | collective-permute-start | bytes 626696 | tf_op jit(solution)/shard_map/ppermute | solution.py:218
  95.1 29.5 %collective-permute-start.19 = (bf16[816,128]{1,0:T(8,128)(2,1)S(1)}, bf16[816,128]{1,0:T(8,128)(2,1)S(1)}, u32[]{:S(2)}, u32[]{:S(2)}) collective-permute-start(bf16[816,128]{1,0:T(8,128)(2,1)S(1)} %pad_maximum_fusion.5), channel_id=1, source_target_pairs={{0,2},{1,3},{2,0},{3,1},{4,6},{5,7},{6,4},{7,5},{8,10},{9,11},{10,... | collective-permute-start | bytes 626696 | tf_op jit(solution)/shard_map/ppermute | solution.py:218
  109.5 17.2 %collective-permute-start.7 = (bf16[816,128]{1,0:T(8,128)(2,1)S(1)}, bf16[816,128]{1,0:T(8,128)(2,1)S(1)}, u32[]{:S(2)}, u32[]{:S(2)}) collective-permute-start(bf16[816,128]{1,0:T(8,128)(2,1)S(1)} %collective-permute-done.5), channel_id=1, source_target_pairs={{2,4},{3,5},{4,2},{5,3},{10,12},{11,13},{12,10},{13,11},{18,20},{1... | collective-permute-start | bytes 626696 | tf_op jit(solution)/shard_map/ppermute | solution.py:218
  110.2 8.3 %collective-permute-start.15 = (bf16[544,128]{1,0:T(8,128)(2,1)S(1)}, bf16[544,128]{1,0:T(8,128)(2,1)S(1)}, u32[]{:S(2)}, u32[]{:S(2)}) collective-permute-start(bf16[544,128]{1,0:T(8,128)(2,1)S(1)} %collective-permute-done.13), channel_id=1, source_target_pairs={{2,0},{3,1},{4,6},{5,7},{10,8},{11,9},{12,14},{13,15},{18,16},{19,... | collective-permute-start | bytes 417800 | tf_op jit(solution)/shard_map/ppermute | solution.py:218
  111.5 14.4 %collective-permute-start.16 = (bf16[544,128]{1,0:T(8,128)(2,1)S(1)}, bf16[544,128]{1,0:T(8,128)(2,1)S(1)}, u32[]{:S(2)}, u32[]{:S(2)}) collective-permute-start(bf16[544,128]{1,0:T(8,128)(2,1)S(1)} %collective-permute-done.14), channel_id=1, source_target_pairs={{2,0},{3,1},{4,6},{5,7},{10,8},{11,9},{12,14},{13,15},{18,16},{19,... | collective-permute-start | bytes 417800 | tf_op jit(solution)/shard_map/ppermute | solution.py:218
  118.5 33.9 %collective-permute-start.1 = (bf16[64,8192]{1,0:T(8,128)(2,1)}, bf16[64,8192]{1,0:T(8,128)(2,1)S(1)}, u32[]{:S(2)}, u32[]{:S(2)}) collective-permute-start(bf16[64,8192]{1,0:T(8,128)(2,1)} %bitcast.37), channel_id=1, source_target_pairs={{64,0},{65,1},{66,2},{67,3},{68,4},{69,5},{70,6},{71,7},{72,8},{73... | collective-permute-start | bytes 3145736 | tf_op jit(solution)/shard_map/ppermute | solution.py:218
  123.3 7.7 %collective-permute-start.8 = (bf16[816,128]{1,0:T(8,128)(2,1)S(1)}, bf16[816,128]{1,0:T(8,128)(2,1)S(1)}, u32[]{:S(2)}, u32[]{:S(2)}) collective-permute-start(bf16[816,128]{1,0:T(8,128)(2,1)S(1)} %collective-permute-done.6), channel_id=1, source_target_pairs={{2,0},{3,1},{4,6},{5,7},{10,8},{11,9},{12,14},{13,15},{18,16},{19,... | collective-permute-start | bytes 626696 | tf_op jit(solution)/shard_map/ppermute | solution.py:218
  124.7 11.1 %copy-start.3 = (bf16[816,128]{1,0:T(8,128)(2,1)}, bf16[816,128]{1,0:T(8,128)(2,1)S(1)}, u32[]{:S(2)}) copy-start(bf16[816,128]{1,0:T(8,128)(2,1)S(1)} %collective-permute-done.19) | copy-start | bytes 626692
  124.7 13.1 %collective-permute-start.22 = (bf16[816,128]{1,0:T(8,128)(2,1)}, bf16[816,128]{1,0:T(8,128)(2,1)S(1)}, u32[]{:S(2)}, u32[]{:S(2)}) collective-permute-start(bf16[816,128]{1,0:T(8,128)(2,1)} %collective-permute-done.20), channel_id=1, source_target_pairs={{2,0},{3,1},{4,6},{5,7},{10,8},{11,9},{12,14},{13,15},{18,16},{19,... | collective-permute-start | bytes 626696 | tf_op jit(solution)/shard_map/ppermute | solution.py:218
  126.0 2.0 %collective-permute-start.21 = (bf16[816,128]{1,0:T(8,128)(2,1)S(1)}, bf16[816,128]{1,0:T(8,128)(2,1)S(1)}, u32[]{:S(2)}, u32[]{:S(2)}) collective-permute-start(bf16[816,128]{1,0:T(8,128)(2,1)S(1)} %collective-permute-done.19), channel_id=1, source_target_pairs={{2,4},{3,5},{4,2},{5,3},{10,12},{11,13},{12,10},{13,11},{18,20},{1... | collective-permute-start | bytes 626696 | tf_op jit(solution)/shard_map/ppermute | solution.py:218
  126.7 9.0 %collective-permute-start.9 = (bf16[816,128]{1,0:T(8,128)(2,1)S(1)}, bf16[816,128]{1,0:T(8,128)(2,1)S(1)}, u32[]{:S(2)}, u32[]{:S(2)}) collective-permute-start(bf16[816,128]{1,0:T(8,128)(2,1)S(1)} %collective-permute-done.7), channel_id=1, source_target_pairs={{2,0},{3,1},{4,6},{5,7},{10,8},{11,9},{12,14},{13,15},{18,16},{19,... | collective-permute-start | bytes 626696 | tf_op jit(solution)/shard_map/ppermute | solution.py:218
  128.0 13.3 %collective-permute-start.23 = (bf16[816,128]{1,0:T(8,128)(2,1)S(1)}, bf16[816,128]{1,0:T(8,128)(2,1)S(1)}, u32[]{:S(2)}, u32[]{:S(2)}) collective-permute-start(bf16[816,128]{1,0:T(8,128)(2,1)S(1)} %collective-permute-done.21), channel_id=1, source_target_pairs={{2,0},{3,1},{4,6},{5,7},{10,8},{11,9},{12,14},{13,15},{18,16},{19,... | collective-permute-start | bytes 626696 | tf_op jit(solution)/shard_map/ppermute | solution.py:218
  135.8 16.6 %collective-permute-start.24 = (bf16[3264,128]{1,0:T(8,128)(2,1)S(1)}, bf16[3264,128]{1,0:T(8,128)(2,1)}, u32[]{:S(2)}, u32[]{:S(2)}) collective-permute-start(bf16[3264,128]{1,0:T(8,128)(2,1)S(1)} %pad_maximum_fusion), channel_id=1, source_target_pairs={{0,1},{1,0},{2,3},{3,2},{4,5},{5,4},{6,7},{7,6},{8,9},{9,8},{10,11... | collective-permute-start | bytes 2506760 | tf_op jit(solution)/shard_map/ppermute | solution.py:218
  141.5 4.9 %copy-start.8 = (f32[1,2]{1,0:T(1,128)S(1)}, f32[1,2]{1,0:T(1,128)}, u32[]{:S(2)}) copy-start(f32[1,2]{1,0:T(1,128)} %param.11) | copy-start | bytes 28
  141.6 10.8 %copy-start = (s32[16]{0:T(128)S(1)}, s32[16]{0:T(128)}, u32[]{:S(2)}) copy-start(s32[16]{0:T(128)} %constant.107.clone.place) | copy-start | bytes 196
  141.6 10.8 %collective-permute-start.26 = (bf16[3264,128]{1,0:T(8,128)(2,1)S(1)}, bf16[3264,128]{1,0:T(8,128)(2,1)}, u32[]{:S(2)}, u32[]{:S(2)}) collective-permute-start(bf16[3264,128]{1,0:T(8,128)(2,1)S(1)} %pad_maximum_fusion.1), channel_id=1, source_target_pairs={{0,1},{1,0},{2,3},{3,2},{4,5},{5,4},{6,7},{7,6},{8,9},{9,8},{10,11... | collective-permute-start | bytes 2506760 | tf_op jit(solution)/shard_map/ppermute | solution.py:218
  143.7 8.7 %collective-permute-start.25 = (bf16[2176,128]{1,0:T(8,128)(2,1)S(1)}, bf16[2176,128]{1,0:T(8,128)(2,1)}, u32[]{:S(2)}, u32[]{:S(2)}) collective-permute-start(bf16[2176,128]{1,0:T(8,128)(2,1)S(1)} %pad_maximum_fusion.3), channel_id=1, source_target_pairs={{0,1},{1,0},{2,3},{3,2},{4,5},{5,4},{6,7},{7,6},{8,9},{9,8},{10,11... | collective-permute-start | bytes 1671176 | tf_op jit(solution)/shard_map/ppermute | solution.py:218
  146.5 5.9 %collective-permute-start = (f32[40,256]{1,0:T(8,128)S(1)}, f32[40,256]{1,0:T(8,128)S(1)}, u32[]{:S(2)}, u32[]{:S(2)}) collective-permute-start(f32[40,256]{1,0:T(8,128)S(1)} %maximum_maximum_fusion), channel_id=1, source_target_pairs={{64,0},{65,1},{66,2},{67,3},{68,4},{69,5},{70,6},{71,7},{72,8},{73... | collective-permute-start | bytes 122888 | tf_op jit(solution)/shard_map/ppermute | solution.py:218
  (5 other events, 17.7 us)
where the time goes:
time: 167 us; the launch traced here: 166 us
  starting transfers between devices  102 us (61%)
  waiting for transfers between devices  46.9 us (28%)
  Pallas kernels  14 us (8%)
  other arithmetic  2.57 us (2%)
    ppermute x27, starting transfers between devices, moved(): return lax.ppermute(value, ('section', 'seq'), shift_pairs(of))  102 us
    ppermute x27, waiting for transfers between devices, moved(): return lax.ppermute(value, ('section', 'seq'), shift_pairs(of))  46.9 us
    pallas_call x1, Pallas kernels, core_call(): pl.pallas_call(functools.partial(core_kernel, seq), out_shape=jax.ShapeDt...  14 us
  transfers between devices with their start and end apart: 27, of which 8 were waited for; matrix products, arithmetic and copies ran while one was open for 1% of the time, Pallas kernels for 0%

commit v1 on v0

--- a/solution.py
+++ b/solution.py
@@ -17,7 +17,7 @@
 DOCS = 16
 STEP_ROWS = 16
 SLAB = 2 * HALF + STEP_ROWS
-UNROLL = 4
+UNROLL = 8
 BASE = (0, 2, 13, 21, 22, 20, 12, 1)
 COUNT = (3, 3, 2, 3, 3, 3, 2, 3)
 FIRST = (0, 12, 20)
@@ -113,13 +113,20 @@
             axis=0,
         )
 
-    def local_of(span, _):
-        _, scaled = grown(span)
-        masked = (scaled * both(keep_ref, span, SPAN)).astype(BF16)
-        local_ref[span] = jnp.dot(masked, rows_of(span, HALF), preferred_element_type=F32)
+    def locals_of(number, _):
+        spans = [number * UNROLL + i for i in range(UNROLL)]
+        ready = [
+            (
+                (grown(span)[1] * both(keep_ref, span, SPAN)).astype(BF16),
+                rows_of(span, HALF),
+            )
+            for span in spans
+        ]
+        for span, (masked, reads) in zip(spans, ready):
+            local_ref[span] = jnp.dot(masked, reads, preferred_element_type=F32)
         return 0
 
-    lax.fori_loop(0, SPANS, local_of, 0, unroll=UNROLL)
+    lax.fori_loop(0, SPANS // UNROLL, locals_of, 0)
 
     def recur(number, state):
         span = SPANS - 1 - number
@@ -143,35 +150,46 @@
     )
     nt = (((1,), (1,)), ((), ()))
 
-    def span_of(span, _):
-        writes = rows_of(span, 0)
-        reads = rows_of(span, HALF)
-        grad, scaled = grown(span)
-        scaled = scaled.astype(BF16)
-        left = jnp.concatenate([reads, right_ref[span]], axis=0)
-        product = lax.dot_general(left, writes, nt, preferred_element_type=F32)
-        carried = product[SPAN : SPAN + 64] + product[SPAN + 64 :]
-        end = end_ref[pl.ds(span, 1), :]
-        first_end, second_end = end[:, :HALF], end[:, HALF:]
-        s00 = jnp.where(behind & (token < first_end), product[:HALF, :HALF], 0.0).astype(BF16)
-        s10 = jnp.where(token + HALF < first_end, product[HALF:SPAN, :HALF], 0.0).astype(BF16)
-        s11 = jnp.where(
-            behind & (token + HALF < second_end), product[HALF:SPAN, HALF:], 0.0
-        ).astype(BF16)
-        zero = jnp.zeros((HALF, HALF), BF16)
-        scores = jnp.concatenate(
-            [jnp.concatenate([s00, zero], axis=1), jnp.concatenate([s10, s11], axis=1)], axis=0
-        )
-        inner = jnp.dot(scaled, scores, preferred_element_type=F32)
-        out = (
-            both(shrink_ref, span, SPAN) * inner
-            + both(carry_ref, span, SPAN) * carried
-            + gains * grad
-        )
-        out_ref[:, pl.ds(pl.multiple_of(span * SPAN, SPAN), SPAN)] = out.astype(BF16)
+    def spans_of(number, _):
+        spans = [number * UNROLL + i for i in range(UNROLL)]
+        left, writes, grads, scaled, ends, shrink, carry = [], [], [], [], [], [], []
+        for span in spans:
+            writes.append(rows_of(span, 0))
+            left.append(jnp.concatenate([rows_of(span, HALF), right_ref[span]], axis=0))
+            grad, grow = grown(span)
+            grads.append(grad)
+            scaled.append(grow.astype(BF16))
+            ends.append(end_ref[pl.ds(span, 1), :])
+            shrink.append(both(shrink_ref, span, SPAN))
+            carry.append(both(carry_ref, span, SPAN))
+        outs = []
+
+        def first_of(i):
+            return lax.dot_general(left[i], writes[i], nt, preferred_element_type=F32)
+
+        ahead_product = first_of(0)
+        for i in range(UNROLL):
+            product = ahead_product
+            if i + 1 < UNROLL:
+                ahead_product = first_of(i + 1)
+            carried = product[SPAN : SPAN + 64] + product[SPAN + 64 :]
+            first_end, second_end = ends[i][:, :HALF], ends[i][:, HALF:]
+            s00 = jnp.where(behind & (token < first_end), product[:HALF, :HALF], 0.0).astype(BF16)
+            s10 = jnp.where(token + HALF < first_end, product[HALF:SPAN, :HALF], 0.0).astype(BF16)
+            s11 = jnp.where(
+                behind & (token + HALF < second_end), product[HALF:SPAN, HALF:], 0.0
+            ).astype(BF16)
+            zero = jnp.zeros((HALF, HALF), BF16)
+            scores = jnp.concatenate(
+                [jnp.concatenate([s00, zero], axis=1), jnp.concatenate([s10, s11], axis=1)], axis=0
+            )
+            inner = jnp.dot(scaled[i], scores, preferred_element_type=F32)
+            outs.append((shrink[i] * inner + carry[i] * carried + gains * grads[i]).astype(BF16))
+        for i, span in enumerate(spans):
+            out_ref[:, pl.ds(pl.multiple_of(span * SPAN, SPAN), SPAN)] = outs[i]
         return 0
 
-    lax.fori_loop(0, SPANS, span_of, 0, unroll=UNROLL)
+    lax.fori_loop(0, SPANS // UNROLL, spans_of, 0)
 
 
 def core_call(small, grad, parts, seq=None, interpret=False):
@@ -230,6 +248,14 @@
     return moved(value, lambda s, g, k, c: (s, g, steps[k], c) if k in steps else None)
 
 
+def level_gather(chunk):
+    chunk = lax.optimization_barrier(chunk)
+    others = [moved(chunk, lambda s, g, k, c, j=j: (s, g, k ^ j, c)) for j in (1, 2, 3)]
+    every = jnp.concatenate((chunk, *others), axis=0)
+    other = moved(every, lambda s, g, k, c: (s, g, k, c ^ 1))
+    return every.reshape(-1, SLAB, STATE), other.reshape(-1, SLAB, STATE)
+
+
 def group_gather(chunk, outer):
     middle, ends = {1: 2, 2: 1}, {1: 0, 2: 3}
     near = levels(chunk, {0: 1, 1: 0, 2: 3, 3: 2})
@@ -241,7 +267,8 @@
         (chunk, near, across, far, end_near, end_far)
     )
     every = jnp.concatenate(
-        [chunk, near, jnp.where(outer, end_near, far), jnp.where(outer, end_far, across)], axis=0
+        [chunk, near, jnp.where(outer, end_near, far), jnp.where(outer, end_far, across)],
+        axis=0,
     )
     other = moved(every, lambda s, g, k, c: (s, g, k, c ^ 1))
     return every.reshape(-1, SLAB, STATE), other.reshape(-1, SLAB, STATE)
@@ -281,8 +308,8 @@
     third_in = jnp.concatenate([right_3[:SLAB], left_3[:SLAB], right_3[SLAB:], left_3[SLAB:]])
     outer = (level == 0) | (level == 3)
     first, first_other = group_gather(first_in, outer)
-    second, second_other = group_gather(second_in, outer)
-    third, third_other = group_gather(third_in, outer)
+    second, second_other = level_gather(second_in)
+    third, third_other = level_gather(third_in)
     out = core_call(
         small, grad, (first, second, third, first_other, second_other, third_other)
     )

time: 167 us -> 168 us (level)
  the two profiles are of different devices: /device:TPU:14 before, /device:TPU:24 now
where the time goes in v1:
time: 168 us; the launch traced here: 166 us
  starting transfers between devices  85.6 us (51%)
  waiting for transfers between devices  67.6 us (40%)
  Pallas kernels  9.63 us (6%)
  other arithmetic  2.45 us (1%)
    ppermute x23, starting transfers between devices, moved(): return lax.ppermute(value, ('section', 'seq'), shift_pairs(of))  85.6 us
    ppermute x23, waiting for transfers between devices, moved(): return lax.ppermute(value, ('section', 'seq'), shift_pairs(of))  67.6 us
    pallas_call x1, Pallas kernels, core_call(): pl.pallas_call(functools.partial(core_kernel, seq), out_shape=jax.ShapeDt...  9.63 us
  transfers between devices with their start and end apart: 23, of which 6 were waited for; matrix products, arithmetic and copies ran while one was open for 0% of the time, Pallas kernels for 0%

profile of v1, /device:TPU:24, one launch (start us, length us, event | category | flops | bytes accessed | tf_op | source)
XLA Modules:
  0.0 166.2 jit_solution(1495887083737013251)
XLA Ops:
  0.0 0.8 convert_element_type.15
  0.8 1.1 pad_maximum_fusion.2
  2.0 2.7 %collective-permute-start.2 = (bf16[272,128]{1,0:T(8,128)(2,1)S(1)}, bf16[272,128]{1,0:T(8,128)(2,1)S(1)}, u32[]{:S(2)}, u32[]{:S(2)}) collective-permute-start(bf16[272,128]{1,0:T(8,128)(2,1)S(1)} %get-tuple-element.23), channel_id=1, source_target_pairs={{64,0},{65,1},{66,2},{67,3},{68,4},{69,5},{70,6},{71,7},{72,8},{73... | collective-permute-start | bytes 208904 | tf_op jit(solution)/shard_map/ppermute | solution.py:236
  4.7 15.6 %collective-permute-start.10 = (bf16[400,128]{1,0:T(8,128)(2,1)S(1)}, bf16[400,128]{1,0:T(8,128)(2,1)S(1)}, u32[]{:S(2)}, u32[]{:S(2)}) collective-permute-start(bf16[400,128]{1,0:T(8,128)(2,1)S(1)} %pad_maximum_fusion.11), channel_id=1, source_target_pairs={{64,16},{65,17},{66,18},{67,19},{68,20},{69,21},{70,22},{71,23},{7... | collective-permute-start | bytes 307208 | tf_op jit(solution)/shard_map/ppermute | solution.py:236
  20.3 9.0 %collective-permute-start.3 = (bf16[544,128]{1,0:T(8,128)(2,1)S(1)}, bf16[544,128]{1,0:T(8,128)(2,1)S(1)}, u32[]{:S(2)}, u32[]{:S(2)}) collective-permute-start(bf16[544,128]{1,0:T(8,128)(2,1)S(1)} %pad_maximum_fusion.6), channel_id=1, source_target_pairs={{64,8},{65,9},{66,10},{67,11},{68,12},{69,13},{70,14},{71,15},{72,... | collective-permute-start | bytes 417800 | tf_op jit(solution)/shard_map/ppermute | solution.py:236
  29.4 4.4 %collective-permute-start.11 = (bf16[416,128]{1,0:T(8,128)(2,1)S(1)}, bf16[416,128]{1,0:T(8,128)(2,1)S(1)}, u32[]{:S(2)}, u32[]{:S(2)}) collective-permute-start(bf16[416,128]{1,0:T(8,128)(2,1)S(1)} %pad_maximum_fusion.9), channel_id=1, source_target_pairs={{64,48},{65,49},{66,50},{67,51},{68,52},{69,53},{70,54},{71,55},{7... | collective-permute-start | bytes 319496 | tf_op jit(solution)/shard_map/ppermute | solution.py:236
  33.8 6.1 %collective-permute-start.4 = (bf16[544,128]{1,0:T(8,128)(2,1)S(1)}, bf16[544,128]{1,0:T(8,128)(2,1)S(1)}, u32[]{:S(2)}, u32[]{:S(2)}) collective-permute-start(bf16[544,128]{1,0:T(8,128)(2,1)S(1)} %pad_maximum_fusion.7), channel_id=1, source_target_pairs={{64,56},{65,57},{66,58},{67,59},{68,60},{69,61},{70,62},{71,63},{7... | collective-permute-start | bytes 417800 | tf_op jit(solution)/shard_map/ppermute | solution.py:236
  39.9 26.0 %collective-permute-done.11 = bf16[416,128]{1,0:T(8,128)(2,1)S(1)} collective-permute-done((bf16[416,128]{1,0:T(8,128)(2,1)S(1)}, bf16[416,128]{1,0:T(8,128)(2,1)S(1)}, u32[]{:S(2)}, u32[]{:S(2)}) %collective-permute-start.11) | collective-permute-done | bytes 106528 | tf_op jit(solution)/shard_map/ppermute | solution.py:236
  66.0 13.6 %collective-permute-start.15 = (bf16[400,128]{1,0:T(8,128)(2,1)S(1)}, bf16[400,128]{1,0:T(8,128)(2,1)S(1)}, u32[]{:S(2)}, u32[]{:S(2)}) collective-permute-start(bf16[400,128]{1,0:T(8,128)(2,1)S(1)} %pad_maximum_fusion.12), channel_id=1, source_target_pairs={{0,16},{1,17},{2,18},{3,19},{4,20},{5,21},{6,22},{7,23},{8,24},{9,... | collective-permute-start | bytes 307208 | tf_op jit(solution)/shard_map/ppermute | solution.py:236
  79.6 1.9 %collective-permute-start.16 = (bf16[416,128]{1,0:T(8,128)(2,1)S(1)}, bf16[416,128]{1,0:T(8,128)(2,1)S(1)}, u32[]{:S(2)}, u32[]{:S(2)}) collective-permute-start(bf16[416,128]{1,0:T(8,128)(2,1)S(1)} %pad_maximum_fusion.10), channel_id=1, source_target_pairs={{0,48},{1,49},{2,50},{3,51},{4,52},{5,53},{6,54},{7,55},{8,56},{9,... | collective-permute-start | bytes 319496 | tf_op jit(solution)/shard_map/ppermute | solution.py:236
  81.6 2.5 %collective-permute-start.5 = (bf16[816,128]{1,0:T(8,128)(2,1)S(1)}, bf16[816,128]{1,0:T(8,128)(2,1)S(1)}, u32[]{:S(2)}, u32[]{:S(2)}) collective-permute-start(bf16[816,128]{1,0:T(8,128)(2,1)S(1)} %pad_maximum_fusion.4), channel_id=1, source_target_pairs={{0,2},{1,3},{2,0},{3,1},{4,6},{5,7},{6,4},{7,5},{8,10},{9,11},{10,... | collective-permute-start | bytes 626696 | tf_op jit(solution)/shard_map/ppermute | solution.py:236
  84.1 0.7 collective-permute-start.6
  84.8 12.5 %collective-permute-done.16 = bf16[416,128]{1,0:T(8,128)(2,1)S(1)} collective-permute-done((bf16[416,128]{1,0:T(8,128)(2,1)S(1)}, bf16[416,128]{1,0:T(8,128)(2,1)S(1)}, u32[]{:S(2)}, u32[]{:S(2)}) %collective-permute-start.16) | collective-permute-done | bytes 106528 | tf_op jit(solution)/shard_map/ppermute | solution.py:236
  97.4 1.9 %collective-permute-start.19 = (bf16[816,128]{1,0:T(8,128)(2,1)S(1)}, bf16[816,128]{1,0:T(8,128)(2,1)S(1)}, u32[]{:S(2)}, u32[]{:S(2)}) collective-permute-start(bf16[816,128]{1,0:T(8,128)(2,1)S(1)} %pad_maximum_fusion.5), channel_id=1, source_target_pairs={{0,6},{1,7},{2,4},{3,5},{4,2},{5,3},{6,0},{7,1},{8,14},{9,15},{10,... | collective-permute-start | bytes 626696 | tf_op jit(solution)/shard_map/ppermute | solution.py:236
  99.3 2.2 %collective-permute-start.18 = (bf16[816,128]{1,0:T(8,128)(2,1)S(1)}, bf16[816,128]{1,0:T(8,128)(2,1)S(1)}, u32[]{:S(2)}, u32[]{:S(2)}) collective-permute-start(bf16[816,128]{1,0:T(8,128)(2,1)S(1)} %pad_maximum_fusion.5), channel_id=1, source_target_pairs={{0,4},{1,5},{2,6},{3,7},{4,0},{5,1},{6,2},{7,3},{8,12},{9,13},{10,... | collective-permute-start | bytes 626696 | tf_op jit(solution)/shard_map/ppermute | solution.py:236
  101.5 6.0 %collective-permute-start.17 = (bf16[816,128]{1,0:T(8,128)(2,1)S(1)}, bf16[816,128]{1,0:T(8,128)(2,1)S(1)}, u32[]{:S(2)}, u32[]{:S(2)}) collective-permute-start(bf16[816,128]{1,0:T(8,128)(2,1)S(1)} %pad_maximum_fusion.5), channel_id=1, source_target_pairs={{0,2},{1,3},{2,0},{3,1},{4,6},{5,7},{6,4},{7,5},{8,10},{9,11},{10,... | collective-permute-start | bytes 626696 | tf_op jit(solution)/shard_map/ppermute | solution.py:236
  107.5 0.7 collective-permute-start.7
  108.3 1.9 %collective-permute-start.1 = (bf16[64,8192]{1,0:T(8,128)(2,1)}, bf16[64,8192]{1,0:T(8,128)(2,1)S(1)}, u32[]{:S(2)}, u32[]{:S(2)}) collective-permute-start(bf16[64,8192]{1,0:T(8,128)(2,1)} %bitcast.37), channel_id=1, source_target_pairs={{64,0},{65,1},{66,2},{67,3},{68,4},{69,5},{70,6},{71,7},{72,8},{73... | collective-permute-start | bytes 3145736 | tf_op jit(solution)/shard_map/ppermute | solution.py:236
  110.2 1.9 %collective-permute-start.14 = (bf16[544,128]{1,0:T(8,128)(2,1)S(1)}, bf16[544,128]{1,0:T(8,128)(2,1)S(1)}, u32[]{:S(2)}, u32[]{:S(2)}) collective-permute-start(bf16[544,128]{1,0:T(8,128)(2,1)S(1)} %pad_maximum_fusion.8), channel_id=1, source_target_pairs={{0,6},{1,7},{2,4},{3,5},{4,2},{5,3},{6,0},{7,1},{8,14},{9,15},{10,... | collective-permute-start | bytes 417800 | tf_op jit(solution)/shard_map/ppermute | solution.py:236
  112.2 11.8 %collective-permute-done.18 = bf16[816,128]{1,0:T(8,128)(2,1)S(1)} collective-permute-done((bf16[816,128]{1,0:T(8,128)(2,1)S(1)}, bf16[816,128]{1,0:T(8,128)(2,1)S(1)}, u32[]{:S(2)}, u32[]{:S(2)}) %collective-permute-start.18) | collective-permute-done | bytes 208928 | tf_op jit(solution)/shard_map/ppermute | solution.py:236
  124.0 1.9 %collective-permute-start.13 = (bf16[544,128]{1,0:T(8,128)(2,1)S(1)}, bf16[544,128]{1,0:T(8,128)(2,1)S(1)}, u32[]{:S(2)}, u32[]{:S(2)}) collective-permute-start(bf16[544,128]{1,0:T(8,128)(2,1)S(1)} %pad_maximum_fusion.8), channel_id=1, source_target_pairs={{0,4},{1,5},{2,6},{3,7},{4,0},{5,1},{6,2},{7,3},{8,12},{9,13},{10,... | collective-permute-start | bytes 417800 | tf_op jit(solution)/shard_map/ppermute | solution.py:236
  125.9 1.3 collective-permute-start.8
  127.2 1.3 collective-permute-start.9
  128.6 9.9 %collective-permute-done.8 = bf16[816,128]{1,0:T(8,128)(2,1)S(1)} collective-permute-done((bf16[816,128]{1,0:T(8,128)(2,1)S(1)}, bf16[816,128]{1,0:T(8,128)(2,1)S(1)}, u32[]{:S(2)}, u32[]{:S(2)}) %collective-permute-start.8) | collective-permute-done | bytes 208928 | tf_op jit(solution)/shard_map/ppermute | solution.py:236
  138.5 1.9 %collective-permute-start.12 = (bf16[544,128]{1,0:T(8,128)(2,1)S(1)}, bf16[544,128]{1,0:T(8,128)(2,1)S(1)}, u32[]{:S(2)}, u32[]{:S(2)}) collective-permute-start(bf16[544,128]{1,0:T(8,128)(2,1)S(1)} %pad_maximum_fusion.8), channel_id=1, source_target_pairs={{0,2},{1,3},{2,0},{3,1},{4,6},{5,7},{6,4},{7,5},{8,10},{9,11},{10,... | collective-permute-start | bytes 417800 | tf_op jit(solution)/shard_map/ppermute | solution.py:236
  140.4 1.3 collective-permute-done.9
  141.7 1.9 %collective-permute-start.22 = (bf16[3264,128]{1,0:T(8,128)(2,1)S(1)}, bf16[3264,128]{1,0:T(8,128)(2,1)}, u32[]{:S(2)}, u32[]{:S(2)}) collective-permute-start(bf16[3264,128]{1,0:T(8,128)(2,1)S(1)} %pad_maximum_fusion.1), channel_id=1, source_target_pairs={{0,1},{1,0},{2,3},{3,2},{4,5},{5,4},{6,7},{7,6},{8,9},{9,8},{10,11... | collective-permute-start | bytes 2506760 | tf_op jit(solution)/shard_map/ppermute | solution.py:236
  143.8 2.4 %collective-permute-start.20 = (bf16[3264,128]{1,0:T(8,128)(2,1)S(1)}, bf16[3264,128]{1,0:T(8,128)(2,1)}, u32[]{:S(2)}, u32[]{:S(2)}) collective-permute-start(bf16[3264,128]{1,0:T(8,128)(2,1)S(1)} %pad_maximum_fusion), channel_id=1, source_target_pairs={{0,1},{1,0},{2,3},{3,2},{4,5},{5,4},{6,7},{7,6},{8,9},{9,8},{10,11... | collective-permute-start | bytes 2506760 | tf_op jit(solution)/shard_map/ppermute | solution.py:236
  146.3 1.9 %collective-permute-start.21 = (bf16[2176,128]{1,0:T(8,128)(2,1)S(1)}, bf16[2176,128]{1,0:T(8,128)(2,1)}, u32[]{:S(2)}, u32[]{:S(2)}) collective-permute-start(bf16[2176,128]{1,0:T(8,128)(2,1)S(1)} %pad_maximum_fusion.3), channel_id=1, source_target_pairs={{0,1},{1,0},{2,3},{3,2},{4,5},{5,4},{6,7},{7,6},{8,9},{9,8},{10,11... | collective-permute-start | bytes 1671176 | tf_op jit(solution)/shard_map/ppermute | solution.py:236
  148.6 1.9 %collective-permute-start = (f32[40,256]{1,0:T(8,128)S(1)}, f32[40,256]{1,0:T(8,128)S(1)}, u32[]{:S(2)}, u32[]{:S(2)}) collective-permute-start(f32[40,256]{1,0:T(8,128)S(1)} %maximum_maximum_fusion), channel_id=1, source_target_pairs={{64,0},{65,1},{66,2},{67,3},{68,4},{69,5},{70,6},{71,7},{72,8},{73... | collective-permute-start | bytes 122888 | tf_op jit(solution)/shard_map/ppermute | solution.py:236
  150.5 6.1 %collective-permute-done.small_ref = f32[40,256]{1,0:T(8,128)S(1)} collective-permute-done((f32[40,256]{1,0:T(8,128)S(1)}, f32[40,256]{1,0:T(8,128)S(1)}, u32[]{:S(2)}, u32[]{:S(2)}) %collective-permute-start) | collective-permute-done | bytes 40992 | tf_op jit(solution)/shard_map/ppermute | solution.py:236
  156.6 9.6 %span_grads.1 = bf16[64,8192]{1,0:T(8,128)(2,1)} custom-call(s32[16]{0:T(128)S(1)} %copy-done, f32[40,256]{1,0:T(8,128)S(1)} %collective-permute-done.small_ref, bf16[64,8192]{1,0:T(8,128)(2,1)S(1)} %collective-permute-done.1.grad_ref, bf16[12,272,128]{2,1,0:T(8,128)(2,1)S(1)} %bitcast.32, bf16[8,272,128]{2,1,0:T(8,128)(2,1)S(1)} %bitcast.33, ...), custom_call_target="tpu_custom_call" | custom-call | tf_op jit(solution)/shard_map/span_grads/pallas_call | solution.py:198
  (61 shorter events, 0.9 us)
Async XLA Ops:
  2.0 79.6 %collective-permute-start.2 = (bf16[272,128]{1,0:T(8,128)(2,1)S(1)}, bf16[272,128]{1,0:T(8,128)(2,1)S(1)}, u32[]{:S(2)}, u32[]{:S(2)}) collective-permute-start(bf16[272,128]{1,0:T(8,128)(2,1)S(1)} %get-tuple-element.23), channel_id=1, source_target_pairs={{64,0},{65,1},{66,2},{67,3},{68,4},{69,5},{70,6},{71,7},{72,8},{73... | collective-permute-start | bytes 208904 | tf_op jit(solution)/shard_map/ppermute | solution.py:236
  4.7 35.2 %collective-permute-start.10 = (bf16[400,128]{1,0:T(8,128)(2,1)S(1)}, bf16[400,128]{1,0:T(8,128)(2,1)S(1)}, u32[]{:S(2)}, u32[]{:S(2)}) collective-permute-start(bf16[400,128]{1,0:T(8,128)(2,1)S(1)} %pad_maximum_fusion.11), channel_id=1, source_target_pairs={{64,16},{65,17},{66,18},{67,19},{68,20},{69,21},{70,22},{71,23},{7... | collective-permute-start | bytes 307208 | tf_op jit(solution)/shard_map/ppermute | solution.py:236
  20.3 45.6 %collective-permute-start.3 = (bf16[544,128]{1,0:T(8,128)(2,1)S(1)}, bf16[544,128]{1,0:T(8,128)(2,1)S(1)}, u32[]{:S(2)}, u32[]{:S(2)}) collective-permute-start(bf16[544,128]{1,0:T(8,128)(2,1)S(1)} %pad_maximum_fusion.6), channel_id=1, source_target_pairs={{64,8},{65,9},{66,10},{67,11},{68,12},{69,13},{70,14},{71,15},{72,... | collective-permute-start | bytes 417800 | tf_op jit(solution)/shard_map/ppermute | solution.py:236
  29.4 36.6 %collective-permute-start.11 = (bf16[416,128]{1,0:T(8,128)(2,1)S(1)}, bf16[416,128]{1,0:T(8,128)(2,1)S(1)}, u32[]{:S(2)}, u32[]{:S(2)}) collective-permute-start(bf16[416,128]{1,0:T(8,128)(2,1)S(1)} %pad_maximum_fusion.9), channel_id=1, source_target_pairs={{64,48},{65,49},{66,50},{67,51},{68,52},{69,53},{70,54},{71,55},{7... | collective-permute-start | bytes 319496 | tf_op jit(solution)/shard_map/ppermute | solution.py:236
  33.8 45.8 %collective-permute-start.4 = (bf16[544,128]{1,0:T(8,128)(2,1)S(1)}, bf16[544,128]{1,0:T(8,128)(2,1)S(1)}, u32[]{:S(2)}, u32[]{:S(2)}) collective-permute-start(bf16[544,128]{1,0:T(8,128)(2,1)S(1)} %pad_maximum_fusion.7), channel_id=1, source_target_pairs={{64,56},{65,57},{66,58},{67,59},{68,60},{69,61},{70,62},{71,63},{7... | collective-permute-start | bytes 417800 | tf_op jit(solution)/shard_map/ppermute | solution.py:236
  66.0 18.8 %collective-permute-start.15 = (bf16[400,128]{1,0:T(8,128)(2,1)S(1)}, bf16[400,128]{1,0:T(8,128)(2,1)S(1)}, u32[]{:S(2)}, u32[]{:S(2)}) collective-permute-start(bf16[400,128]{1,0:T(8,128)(2,1)S(1)} %pad_maximum_fusion.12), channel_id=1, source_target_pairs={{0,16},{1,17},{2,18},{3,19},{4,20},{5,21},{6,22},{7,23},{8,24},{9,... | collective-permute-start | bytes 307208 | tf_op jit(solution)/shard_map/ppermute | solution.py:236
  79.6 17.7 %collective-permute-start.16 = (bf16[416,128]{1,0:T(8,128)(2,1)S(1)}, bf16[416,128]{1,0:T(8,128)(2,1)S(1)}, u32[]{:S(2)}, u32[]{:S(2)}) collective-permute-start(bf16[416,128]{1,0:T(8,128)(2,1)S(1)} %pad_maximum_fusion.10), channel_id=1, source_target_pairs={{0,48},{1,49},{2,50},{3,51},{4,52},{5,53},{6,54},{7,55},{8,56},{9,... | collective-permute-start | bytes 319496 | tf_op jit(solution)/shard_map/ppermute | solution.py:236
  81.6 25.9 %collective-permute-start.5 = (bf16[816,128]{1,0:T(8,128)(2,1)S(1)}, bf16[816,128]{1,0:T(8,128)(2,1)S(1)}, u32[]{:S(2)}, u32[]{:S(2)}) collective-permute-start(bf16[816,128]{1,0:T(8,128)(2,1)S(1)} %pad_maximum_fusion.4), channel_id=1, source_target_pairs={{0,2},{1,3},{2,0},{3,1},{4,6},{5,7},{6,4},{7,5},{8,10},{9,11},{10,... | collective-permute-start | bytes 626696 | tf_op jit(solution)/shard_map/ppermute | solution.py:236
  84.1 24.2 %collective-permute-start.6 = (bf16[816,128]{1,0:T(8,128)(2,1)S(1)}, bf16[816,128]{1,0:T(8,128)(2,1)S(1)}, u32[]{:S(2)}, u32[]{:S(2)}) collective-permute-start(bf16[816,128]{1,0:T(8,128)(2,1)S(1)} %pad_maximum_fusion.4), channel_id=1, source_target_pairs={{2,4},{3,5},{4,2},{5,3},{10,12},{11,13},{12,10},{13,11},{18,20},{1... | collective-permute-start | bytes 626696 | tf_op jit(solution)/shard_map/ppermute | solution.py:236
  97.4 12.9 %collective-permute-start.19 = (bf16[816,128]{1,0:T(8,128)(2,1)S(1)}, bf16[816,128]{1,0:T(8,128)(2,1)S(1)}, u32[]{:S(2)}, u32[]{:S(2)}) collective-permute-start(bf16[816,128]{1,0:T(8,128)(2,1)S(1)} %pad_maximum_fusion.5), channel_id=1, source_target_pairs={{0,6},{1,7},{2,4},{3,5},{4,2},{5,3},{6,0},{7,1},{8,14},{9,15},{10,... | collective-permute-start | bytes 626696 | tf_op jit(solution)/shard_map/ppermute | solution.py:236
  99.3 24.7 %collective-permute-start.18 = (bf16[816,128]{1,0:T(8,128)(2,1)S(1)}, bf16[816,128]{1,0:T(8,128)(2,1)S(1)}, u32[]{:S(2)}, u32[]{:S(2)}) collective-permute-start(bf16[816,128]{1,0:T(8,128)(2,1)S(1)} %pad_maximum_fusion.5), channel_id=1, source_target_pairs={{0,4},{1,5},{2,6},{3,7},{4,0},{5,1},{6,2},{7,3},{8,12},{9,13},{10,... | collective-permute-start | bytes 626696 | tf_op jit(solution)/shard_map/ppermute | solution.py:236
  101.5 24.4 %collective-permute-start.17 = (bf16[816,128]{1,0:T(8,128)(2,1)S(1)}, bf16[816,128]{1,0:T(8,128)(2,1)S(1)}, u32[]{:S(2)}, u32[]{:S(2)}) collective-permute-start(bf16[816,128]{1,0:T(8,128)(2,1)S(1)} %pad_maximum_fusion.5), channel_id=1, source_target_pairs={{0,2},{1,3},{2,0},{3,1},{4,6},{5,7},{6,4},{7,5},{8,10},{9,11},{10,... | collective-permute-start | bytes 626696 | tf_op jit(solution)/shard_map/ppermute | solution.py:236
  107.5 19.7 %copy-start.1 = (bf16[816,128]{1,0:T(8,128)(2,1)}, bf16[816,128]{1,0:T(8,128)(2,1)S(1)}, u32[]{:S(2)}) copy-start(bf16[816,128]{1,0:T(8,128)(2,1)S(1)} %collective-permute-done.5) | copy-start | bytes 626692
  107.5 19.7 %collective-permute-start.7 = (bf16[816,128]{1,0:T(8,128)(2,1)S(1)}, bf16[816,128]{1,0:T(8,128)(2,1)S(1)}, u32[]{:S(2)}, u32[]{:S(2)}) collective-permute-start(bf16[816,128]{1,0:T(8,128)(2,1)S(1)} %collective-permute-done.5), channel_id=1, source_target_pairs={{2,4},{3,5},{4,2},{5,3},{10,12},{11,13},{12,10},{13,11},{18,20},{1... | collective-permute-start | bytes 626696 | tf_op jit(solution)/shard_map/ppermute | solution.py:236
  108.3 48.3 %collective-permute-start.1 = (bf16[64,8192]{1,0:T(8,128)(2,1)}, bf16[64,8192]{1,0:T(8,128)(2,1)S(1)}, u32[]{:S(2)}, u32[]{:S(2)}) collective-permute-start(bf16[64,8192]{1,0:T(8,128)(2,1)} %bitcast.37), channel_id=1, source_target_pairs={{64,0},{65,1},{66,2},{67,3},{68,4},{69,5},{70,6},{71,7},{72,8},{73... | collective-permute-start | bytes 3145736 | tf_op jit(solution)/shard_map/ppermute | solution.py:236
  110.2 33.6 %collective-permute-start.14 = (bf16[544,128]{1,0:T(8,128)(2,1)S(1)}, bf16[544,128]{1,0:T(8,128)(2,1)S(1)}, u32[]{:S(2)}, u32[]{:S(2)}) collective-permute-start(bf16[544,128]{1,0:T(8,128)(2,1)S(1)} %pad_maximum_fusion.8), channel_id=1, source_target_pairs={{0,6},{1,7},{2,4},{3,5},{4,2},{5,3},{6,0},{7,1},{8,14},{9,15},{10,... | collective-permute-start | bytes 417800 | tf_op jit(solution)/shard_map/ppermute | solution.py:236
  124.0 22.3 %collective-permute-start.13 = (bf16[544,128]{1,0:T(8,128)(2,1)S(1)}, bf16[544,128]{1,0:T(8,128)(2,1)S(1)}, u32[]{:S(2)}, u32[]{:S(2)}) collective-permute-start(bf16[544,128]{1,0:T(8,128)(2,1)S(1)} %pad_maximum_fusion.8), channel_id=1, source_target_pairs={{0,4},{1,5},{2,6},{3,7},{4,0},{5,1},{6,2},{7,3},{8,12},{9,13},{10,... | collective-permute-start | bytes 417800 | tf_op jit(solution)/shard_map/ppermute | solution.py:236
  125.9 12.6 %collective-permute-start.8 = (bf16[816,128]{1,0:T(8,128)(2,1)S(1)}, bf16[816,128]{1,0:T(8,128)(2,1)S(1)}, u32[]{:S(2)}, u32[]{:S(2)}) collective-permute-start(bf16[816,128]{1,0:T(8,128)(2,1)S(1)} %collective-permute-done.6), channel_id=1, source_target_pairs={{2,0},{3,1},{4,6},{5,7},{10,8},{11,9},{12,14},{13,15},{18,16},{19,... | collective-permute-start | bytes 626696 | tf_op jit(solution)/shard_map/ppermute | solution.py:236
  127.2 14.5 %collective-permute-start.9 = (bf16[816,128]{1,0:T(8,128)(2,1)S(1)}, bf16[816,128]{1,0:T(8,128)(2,1)S(1)}, u32[]{:S(2)}, u32[]{:S(2)}) collective-permute-start(bf16[816,128]{1,0:T(8,128)(2,1)S(1)} %collective-permute-done.7), channel_id=1, source_target_pairs={{2,0},{3,1},{4,6},{5,7},{10,8},{11,9},{12,14},{13,15},{18,16},{19,... | collective-permute-start | bytes 626696 | tf_op jit(solution)/shard_map/ppermute | solution.py:236
  128.5 15.2 %copy-start.2 = (bf16[816,128]{1,0:T(8,128)(2,1)S(1)}, bf16[816,128]{1,0:T(8,128)(2,1)}, u32[]{:S(2)}) copy-start(bf16[816,128]{1,0:T(8,128)(2,1)} %copy-done.1) | copy-start | bytes 626692
  138.5 7.8 %collective-permute-start.12 = (bf16[544,128]{1,0:T(8,128)(2,1)S(1)}, bf16[544,128]{1,0:T(8,128)(2,1)S(1)}, u32[]{:S(2)}, u32[]{:S(2)}) collective-permute-start(bf16[544,128]{1,0:T(8,128)(2,1)S(1)} %pad_maximum_fusion.8), channel_id=1, source_target_pairs={{0,2},{1,3},{2,0},{3,1},{4,6},{5,7},{6,4},{7,5},{8,10},{9,11},{10,... | collective-permute-start | bytes 417800 | tf_op jit(solution)/shard_map/ppermute | solution.py:236
  141.7 14.9 %collective-permute-start.22 = (bf16[3264,128]{1,0:T(8,128)(2,1)S(1)}, bf16[3264,128]{1,0:T(8,128)(2,1)}, u32[]{:S(2)}, u32[]{:S(2)}) collective-permute-start(bf16[3264,128]{1,0:T(8,128)(2,1)S(1)} %pad_maximum_fusion.1), channel_id=1, source_target_pairs={{0,1},{1,0},{2,3},{3,2},{4,5},{5,4},{6,7},{7,6},{8,9},{9,8},{10,11... | collective-permute-start | bytes 2506760 | tf_op jit(solution)/shard_map/ppermute | solution.py:236
  143.7 4.5 %copy-start.3 = (s32[1,8192]{1,0:T(1,128)S(1)}, s32[1,8192]{1,0:T(1,128)}, u32[]{:S(2)}) copy-start(s32[1,8192]{1,0:T(1,128)} %param.14) | copy-start | bytes 98308
  143.7 4.7 %copy-start.4 = (f32[1,2]{1,0:T(1,128)S(1)}, f32[1,2]{1,0:T(1,128)}, u32[]{:S(2)}) copy-start(f32[1,2]{1,0:T(1,128)} %param.11) | copy-start | bytes 28
  143.7 4.7 %copy-start.5 = (f32[1,2]{1,0:T(1,128)S(1)}, f32[1,2]{1,0:T(1,128)}, u32[]{:S(2)}) copy-start(f32[1,2]{1,0:T(1,128)} %param.10) | copy-start | bytes 28
  143.8 12.8 %copy-start = (s32[16]{0:T(128)S(1)}, s32[16]{0:T(128)}, u32[]{:S(2)}) copy-start(s32[16]{0:T(128)} %constant.107.clone.place) | copy-start | bytes 196
  143.8 12.8 %collective-permute-start.20 = (bf16[3264,128]{1,0:T(8,128)(2,1)S(1)}, bf16[3264,128]{1,0:T(8,128)(2,1)}, u32[]{:S(2)}, u32[]{:S(2)}) collective-permute-start(bf16[3264,128]{1,0:T(8,128)(2,1)S(1)} %pad_maximum_fusion), channel_id=1, source_target_pairs={{0,1},{1,0},{2,3},{3,2},{4,5},{5,4},{6,7},{7,6},{8,9},{9,8},{10,11... | collective-permute-start | bytes 2506760 | tf_op jit(solution)/shard_map/ppermute | solution.py:236
  146.3 10.3 %collective-permute-start.21 = (bf16[2176,128]{1,0:T(8,128)(2,1)S(1)}, bf16[2176,128]{1,0:T(8,128)(2,1)}, u32[]{:S(2)}, u32[]{:S(2)}) collective-permute-start(bf16[2176,128]{1,0:T(8,128)(2,1)S(1)} %pad_maximum_fusion.3), channel_id=1, source_target_pairs={{0,1},{1,0},{2,3},{3,2},{4,5},{5,4},{6,7},{7,6},{8,9},{9,8},{10,11... | collective-permute-start | bytes 1671176 | tf_op jit(solution)/shard_map/ppermute | solution.py:236
  148.6 8.0 %collective-permute-start = (f32[40,256]{1,0:T(8,128)S(1)}, f32[40,256]{1,0:T(8,128)S(1)}, u32[]{:S(2)}, u32[]{:S(2)}) collective-permute-start(f32[40,256]{1,0:T(8,128)S(1)} %maximum_maximum_fusion), channel_id=1, source_target_pairs={{64,0},{65,1},{66,2},{67,3},{68,4},{69,5},{70,6},{71,7},{72,8},{73... | collective-permute-start | bytes 122888 | tf_op jit(solution)/shard_map/ppermute | solution.py:236
